TPU v7x, 128 devices: a whole 4x4x4 slice. The times are simulated.
128 devices in a mesh: occ: 4 (over x_lo, core), blk: 32 (over y, z, x_hi).
Axes of the slice: x: 4 (x_hi: 2, x_lo: 2; x = x_hi * 2 + x_lo), y: 4, z: 4, core: 2. Of those that a mesh axis runs over, the one named last changes fastest.
Arguments:
- half_rows: float32 [12, 4096, 3072], P(None, ('occ', 'blk')), may hold values from -6 to 6
- screen: int32 [12, 512], P(None, ('occ', 'blk')), may hold values 0 or 1
- slot_shell: int32 [512], replicated, may hold values from -1 to 143, as said below
- vir_coeff: float32 [1152, 1024], replicated, may hold values from -0.0234375 to 0.0234375
- occ_energy: float32 [12], P('occ'), may hold values from -2 to -0.3
- vir_energy: float32 [1024], P('blk'), may hold values from 0.1 to 3
- pair_list: int32 [24, 2], P('occ'), may hold values from 0 to 2, as said below
Outputs:
- gamma: float32 [12, 1024, 3072], P('occ', 'blk')
Inputs may be any that keep to these rules, and one draw needn't show every extreme that they name: `slot_shell`: every shell block 0 to 143 stands in exactly one slot; -1 marks an empty slot; some owner has all 4 of its slots filled. `pair_list`: the 6 entries of each group are distinct ordered pairs.
All inputs are finite; a program needn't handle non-finite values. No bound on the sum of `screen` on one device may be relied on, other than what follows from the above.
Results may differ from a plain program's by a relative error of at most 0.0001.
Values sent between devices are 32-bit elements; how exact they have to be, the bound alone decides.
No kernel may reach another device: no remote copies, remote signals or barrier semaphores. Data moves between devices by JAX's collectives and lax.ppermute only.
A program may use at most 128 MiB of HBM per device.

v0:
```python
import jax
import jax.numpy as jnp
from jax import lax
from jax.experimental import pallas as pl
from jax.experimental.pallas import tpu as pltpu
from jax.sharding import Mesh, PartitionSpec as P

NVIR = 1024
SHW = 8
NSH = 144
ROWS = NSH * SHW
AUX = 3072
ALL = ("xl", "co", "y", "z", "xh")
GROUP = ("y", "z", "xh")
DEPTH = 1536
VLIM = 60 * 1024 * 1024
f32 = jnp.float32
bf16 = jnp.bfloat16


def params():
    return pltpu.CompilerParams(vmem_limit_bytes=VLIM)


def swap4(v):
    lane = lax.broadcasted_iota(jnp.int32, v[0].shape, 1)
    low = lane < 64
    even = (lane // 32) % 2 == 0
    a0 = jnp.where(low, v[0], pltpu.roll(v[2], 64, 1))
    a2 = jnp.where(low, pltpu.roll(v[0], 64, 1), v[2])
    a1 = jnp.where(low, v[1], pltpu.roll(v[3], 64, 1))
    a3 = jnp.where(low, pltpu.roll(v[1], 64, 1), v[3])
    w0 = jnp.where(even, a0, pltpu.roll(a1, 32, 1))
    w1 = jnp.where(even, pltpu.roll(a0, 96, 1), a1)
    w2 = jnp.where(even, a2, pltpu.roll(a3, 32, 1))
    w3 = jnp.where(even, pltpu.roll(a2, 96, 1), a3)
    return w0, w1, w2, w3


def mix4(v):
    lane = lax.broadcasted_iota(jnp.int32, v[0].shape, 1)
    low = lane < 64
    first = lane < 32
    third = lane < 96
    out = []
    for q in range(4):
        p = [v[(n - q) % 4] for n in range(4)]
        out.append(jnp.where(low, jnp.where(first, p[0], p[1]), jnp.where(third, p[2], p[3])))
    return out


def split(x):
    hi = x.astype(bf16)
    lo = (x - hi.astype(f32)).astype(bf16)
    return hi, lo


def map_kernel(me_ref, row_ref, col_ref, o_ref):
    def parts(g):
        owner = g // 4
        chip = owner // 64 * 32 + owner % 32
        return chip, owner // 32 % 2 * 4 + g % 4

    here, at = parts(lax.broadcasted_iota(jnp.int32, (512, 1), 0))
    there, other = parts(lax.broadcasted_iota(jnp.int32, (1, 512), 1))
    taken = (row_ref[...] >= 0).astype(jnp.int32)
    mates = jnp.where(here == there, taken, 0)
    count = jnp.sum(mates, axis=1, keepdims=True)
    rank = jnp.sum(jnp.where(other < at, mates, 0), axis=1, keepdims=True)
    shell = col_ref[...]
    lane = lax.broadcasted_iota(jnp.int32, (1, 256), 1)
    place = jnp.sum(jnp.where(shell == lane, here * 8 + rank, 0), axis=0, keepdims=True)
    mine = (here == me_ref[0]) & (shell >= 0) & (rank == lane)
    order = jnp.sum(jnp.where(mine, at, 0), axis=0, keepdims=True)
    most = jnp.max(count, axis=0, keepdims=True)
    o_ref[...] = jnp.zeros_like(o_ref)
    o_ref[0:1, :] = place
    o_ref[1:2, :] = order
    o_ref[2:3, :] = jnp.broadcast_to(most, (1, 256))


def slot_map(me, slot_shell):
    vmem = pl.BlockSpec(memory_space=pltpu.VMEM)
    return pl.pallas_call(
        map_kernel,
        in_specs=[pl.BlockSpec(memory_space=pltpu.SMEM), vmem, vmem],
        out_shape=jax.ShapeDtypeStruct((8, 256), jnp.int32),
        compiler_params=pltpu.CompilerParams(vmem_limit_bytes=16 * 1024 * 1024),
        name="slot_map",
    )(me, slot_shell.reshape(1, 512), slot_shell.reshape(512, 1))


def gift_kernel(me_ref, scr_ref, x_ref, o_ref, buf, in_sem, out_sem):
    co = me_ref[1]
    into = []
    for g in range(2):
        for i in range(3):
            n = 3 * g + i
            into.append(pltpu.make_async_copy(x_ref.at[g, 1 - co, 32 * i : 32 * i + 32], buf.at[n], in_sem.at[n]))
            into[n].start()
    out = []
    for g in range(2):
        for i in range(3):
            n = 3 * g + i
            into[n].wait()
            for s in range(4):
                keep = scr_ref[s, (2 * g + 1 - co) * 3 + i].astype(f32)
                buf[n, 8 * s : 8 * s + 8, :] = buf[n, 8 * s : 8 * s + 8, :] * keep
            out.append(pltpu.make_async_copy(buf.at[n], o_ref.at[g, 32 * i : 32 * i + 32], out_sem.at[n]))
            out[n].start()
    for copy in out:
        copy.wait()


def gift(me, screen_t, rows):
    smem = pl.BlockSpec(memory_space=pltpu.SMEM)
    hbm = pl.BlockSpec(memory_space=pl.ANY)
    return pl.pallas_call(
        gift_kernel,
        in_specs=[smem, smem, hbm],
        out_specs=hbm,
        out_shape=jax.ShapeDtypeStruct((2, 96, AUX), f32),
        scratch_shapes=[
            pltpu.VMEM((6, 32, AUX), f32),
            pltpu.SemaphoreType.DMA((6,)),
            pltpu.SemaphoreType.DMA((6,)),
        ],
        compiler_params=pltpu.CompilerParams(vmem_limit_bytes=16 * 1024 * 1024),
        name="gift_rows",
    )(me, screen_t, rows)


def energy_at(cap):
    return 16 * cap + 8 * (cap // 4)


def message_rows(cap):
    return energy_at(cap) + 8


def pack_kernel(cap, me_ref, scr_ref, map_ref, e_ref, x_hbm, y_hbm, o_hbm, x_ref, y_ref, o_ref, in_sem, out_sem):
    co = me_ref[1]

    def into(m):
        at = pl.ds(pl.multiple_of(384 * m, 384), 384)
        return (
            pltpu.make_async_copy(x_hbm.at[:, co, :, at], x_ref.at[m], in_sem.at[0, m]),
            pltpu.make_async_copy(y_hbm.at[:, :, at], y_ref.at[m], in_sem.at[1, m]),
        )

    def out(m):
        return pltpu.make_async_copy(o_ref.at[m], o_hbm.at[:, pl.ds(4 * m, 4)], out_sem.at[m])

    for m in range(8):
        for copy in into(m):
            copy.start()

    def body(m, carry):
        for copy in into(m):
            copy.wait()
        for g in range(2):

            def part(p, i, t):
                place = map_ref[1, p]
                s = place % 4
                at = pl.ds(pl.multiple_of(32 * i + 8 * s, 8), 8)
                cols = slice(128 * t, 128 * t + 128)
                keep = scr_ref[s, (2 * g + co) * 3 + i].astype(f32)
                return jnp.where(place // 4 == co, x_ref[m, g, at, cols] * keep, y_ref[m, g, at, cols])

            for p in range(cap):
                for u in range(2):
                    w = mix4([part(p, *divmod(4 * u + h, 3)) for h in range(4)])
                    for q in range(4):
                        o_ref[m, g, q, 8 * (2 * p + u) : 8 * (2 * p + u) + 8, :] = w[q]
            for four in range((cap + 3) // 4):
                w = swap4([part(min(4 * four + n, cap - 1), 2, 2) for n in range(4)])
                to = 16 * cap + 8 * four
                for q in range(4):
                    o_ref[m, g, q, to : to + 8, :] = jnp.where(tail, energy, w[q]) if to == energy_at(cap) else w[q]
            if cap % 4 == 0:
                for q in range(4):
                    o_ref[m, g, q, energy_at(cap) : energy_at(cap) + 8, :] = energy
        out(m).start()
        return carry

    tail = lax.broadcasted_iota(jnp.int32, (8, 128), 1) >= 96
    energy = jnp.broadcast_to(e_ref[...], (8, 128))
    lax.fori_loop(0, 8, body, 0)
    for m in range(8):
        out(m).wait()


def pack(cap, me, screen_t, meta, energy_row, rows, given):
    size = message_rows(cap)

    def body(*refs):
        pack_kernel(cap, *refs)

    smem = pl.BlockSpec(memory_space=pltpu.SMEM)
    hbm = pl.BlockSpec(memory_space=pl.ANY)
    return pl.pallas_call(
        body,
        in_specs=[smem, smem, smem, pl.BlockSpec(memory_space=pltpu.VMEM), hbm, hbm],
        out_specs=pl.BlockSpec(memory_space=pltpu.HBM),
        out_shape=jax.ShapeDtypeStruct((2, 32, size, 128), f32),
        scratch_shapes=[
            pltpu.VMEM((8, 2, 96, 384), f32),
            pltpu.VMEM((8, 2, 96, 384), f32),
            pltpu.VMEM((8, 2, 4, size, 128), f32),
            pltpu.SemaphoreType.DMA((2, 8)),
            pltpu.SemaphoreType.DMA((8,)),
        ],
        compiler_params=pltpu.CompilerParams(vmem_limit_bytes=60 * 1024 * 1024),
        name=f"pack_rows_{cap}",
    )(me, screen_t, meta, energy_row, rows, given)


def coeff_kernel(c_ref, hi_ref, lo_ref):
    hi, lo = split(c_ref[...].T)
    hi_ref[...] = hi
    lo_ref[...] = lo


def coeff(vir_coeff):
    return pl.pallas_call(
        coeff_kernel,
        grid=(9,),
        in_specs=[pl.BlockSpec((128, NVIR), lambda k: (k, 0))],
        out_specs=[pl.BlockSpec((NVIR, 128), lambda k: (0, k))] * 2,
        out_shape=[jax.ShapeDtypeStruct((NVIR, ROWS), bf16)] * 2,
        compiler_params=params(),
        name="split_coeff",
    )(vir_coeff)


SHARDS = (
    (0, 0, 0), (1, 0, 0), (3, 0, 0), (2, 0, 0),
    (0, 0, 0), (0, 1, 0), (0, 3, 0), (0, 0, 1), (0, 2, 0), (0, 1, 1), (0, 3, 1), (0, 2, 1),
)


def transform_kernel(cap, me_ref, map_ref, r_hbm, chi_ref, clo_ref, o_ref, e_ref, r_ref, xs, sem):
    @pl.when(pl.program_id(0) == 0)
    def _():
        copies = [
            pltpu.make_async_copy(r_hbm.at[16 * n : 16 * n + 16], r_ref.at[16 * n : 16 * n + 16], sem.at[n])
            for n in range(4)
        ]
        for copy in copies:
            copy.start()
        for copy in copies:
            copy.wait()
        blk = me_ref[0] % 32
        y, z, xh = blk // 8, blk // 2 % 4, blk % 2
        lanes = lax.broadcasted_iota(jnp.int32, (1, 128), 1)
        for n, (dy, dz, dx) in enumerate(SHARDS):
            at = (y + dy) % 4 * 8 + (z + dz) % 4 * 2 + (xh + dx) % 2
            line = jnp.where(lanes >= 96, r_ref[at, energy_at(cap) : energy_at(cap) + 1, :], 0.0)
            line += pltpu.roll(line, 64, 1)
            line += pltpu.roll(line, 32, 1)
            e_ref[n : n + 1, :] = line
        quarter = lax.broadcasted_iota(jnp.int32, (8, 128), 1) // 32

        def body(h, carry):
            tiles = []
            for e in range(2):
                where = map_ref[0, 2 * h + e]
                chip = where // 8
                rank = where % 8
                t01 = r_ref[chip, pl.ds(pl.multiple_of(rank * 16, 16), 16), :]
                t2 = r_ref[chip, pl.ds(pl.multiple_of(16 * cap + rank // 4 * 8, 8), 8), :]
                t2 = jnp.where(quarter == rank % 4, t2, 0.0)
                tiles.append((t01[:8], t01[8:], t2))
            row = pl.multiple_of(h * 16, 16)
            for n in range(3):
                hi, lo = split(jnp.concatenate([tiles[0][n], tiles[1][n]], axis=0))
                xs[pl.ds(row, 16), 128 * n : 128 * n + 128] = hi
                xs[pl.ds(row, 16), 384 + 128 * n : 512 + 128 * n] = lo
            return carry

        lax.fori_loop(0, NSH // 2, body, 0, unroll=4)

    both = jnp.dot(chi_ref[...], xs[...], preferred_element_type=f32)
    y = both[:, :384] + both[:, 384:]
    y += jnp.dot(clo_ref[...], xs[:, :384], preferred_element_type=f32)
    lane = lax.broadcasted_iota(jnp.int32, (8, 128), 1) // 32
    for k in range(16):
        last = jnp.zeros((8, 128), f32)
        for ag in range(4):
            rows = slice(32 * k + 8 * ag, 32 * k + 8 * ag + 8)
            for u in range(2):
                o_ref[k, 8 * (2 * ag + u) : 8 * (2 * ag + u) + 8, :] = y[rows, 128 * u : 128 * u + 128]
            piece = y[rows, 256:384]
            piece += pltpu.roll(piece, 64, 1)
            piece += pltpu.roll(piece, 32, 1)
            last = jnp.where(lane == ag, piece, last)
        o_ref[k, 64:72, :] = last


def transform(cap, me, meta, rows, chi, clo):
    def body(*refs):
        transform_kernel(cap, *refs)

    return pl.pallas_call(
        body,
        grid=(2,),
        in_specs=[
            pl.BlockSpec(memory_space=pltpu.SMEM),
            pl.BlockSpec(memory_space=pltpu.SMEM),
            pl.BlockSpec(memory_space=pl.ANY),
            pl.BlockSpec((512, ROWS), lambda m: (m, 0)),
            pl.BlockSpec((512, ROWS), lambda m: (m, 0)),
        ],
        out_specs=[pl.BlockSpec((16, 72, 128), lambda m: (m, 0, 0)), pl.BlockSpec((12, 128), lambda m: (0, 0))],
        out_shape=[jax.ShapeDtypeStruct((32, 72, 128), f32), jax.ShapeDtypeStruct((12, 128), f32)],
        scratch_shapes=[
            pltpu.VMEM((64, message_rows(cap), 128), f32),
            pltpu.VMEM((ROWS, 768), bf16),
            pltpu.SemaphoreType.DMA((4,)),
        ],
        compiler_params=pltpu.CompilerParams(vmem_limit_bytes=36 * 1024 * 1024),
        name=f"transform_rows_{cap}",
    )(me, meta, rows, chi, clo)


def unpack_kernel(q_hbm, f_hbm, q_ref, f_ref, in_sem, out_sem):
    def into(m):
        at = pl.ds(4 * m, 4)
        return pltpu.make_async_copy(q_hbm.at[at], q_ref.at[at], in_sem.at[m])

    def out(m):
        at = pl.ds(pl.multiple_of(384 * m, 384), 384)
        return pltpu.make_async_copy(f_ref.at[:, at], f_hbm.at[:, at], out_sem.at[m])

    for m in range(8):
        into(m).start()

    def body(m, carry):
        into(m).wait()
        for ag in range(4):
            for u in range(2):
                w = mix4([q_ref[4 * m + q, 8 * (2 * ag + u) : 8 * (2 * ag + u) + 8, :] for q in range(4)])
                for h in range(4):
                    i, t = divmod(4 * u + h, 3)
                    at = pl.multiple_of(384 * m + 128 * t, 128)
                    f_ref[32 * i + 8 * ag : 32 * i + 8 * ag + 8, pl.ds(at, 128)] = w[h]
        w = swap4([q_ref[4 * m + q, 64:72, :] for q in range(4)])
        at = pl.multiple_of(384 * m + 256, 128)
        for ag in range(4):
            f_ref[64 + 8 * ag : 64 + 8 * ag + 8, pl.ds(at, 128)] = w[ag]
        out(m).start()
        return carry

    lax.fori_loop(0, 8, body, 0)
    for m in range(8):
        out(m).wait()


def unpack(received):
    hbm = pl.BlockSpec(memory_space=pl.ANY)
    return pl.pallas_call(
        unpack_kernel,
        in_specs=[hbm],
        out_specs=hbm,
        out_shape=jax.ShapeDtypeStruct((96, AUX), f32),
        scratch_shapes=[
            pltpu.VMEM((32, 72, 128), f32),
            pltpu.VMEM((96, AUX), f32),
            pltpu.SemaphoreType.DMA((8,)),
            pltpu.SemaphoreType.DMA((8,)),
        ],
        compiler_params=pltpu.CompilerParams(vmem_limit_bytes=16 * 1024 * 1024),
        name="unpack_fitted",
    )(received)


def block_kernel(n_a, n_b, n_acc, n_out, shards, row_at, col_at, *refs):
    pairs_ref, oe_ref, e_ref = refs[:3]
    a_refs = refs[3 : 3 + n_a]
    b_refs = refs[3 + n_a : 3 + n_a + n_b]
    acc_refs = refs[3 + n_a + n_b : 3 + n_a + n_b + n_acc]
    outs = refs[3 + n_a + n_b + n_acc : 3 + n_a + n_b + n_acc + n_out]
    a_in, b_in, g_buf, ahi, alo, bst, c_ref, whi, wlo, a_sem, b_sem, acc_sem, out_sem = refs[-13:]
    wide = shards > 1
    width = 384 if wide else 128
    rows_total = ahi.shape[0]

    def into(group, buf, sem):
        copies = []
        row = 0
        for n, ref in enumerate(group):
            h = ref.shape[0]
            copies.append((pltpu.make_async_copy(ref, buf.at[row : row + h], sem.at[n]), row, h))
            row += h
        for copy, _, _ in copies:
            copy.start()
        return copies

    a_copies = into(a_refs, a_in, a_sem)
    b_copies = into(b_refs, b_in, b_sem)
    acc_copies = into(acc_refs, g_buf, acc_sem)
    for copy, row, h in a_copies:
        copy.wait()
        for r in range(row, row + h, 16):
            hi, lo = split(a_in[r : r + 16, :])
            ahi[r : r + 16, :] = hi
            alo[r : r + 16, :] = lo
    for copy, row, h in b_copies:
        copy.wait()
        for r in range(row, row + h, 32):
            shard, j = divmod(r // 32, 3)
            hi, lo = split(b_in[r : r + 32, :])
            to = 128 * j + 32 * shard if wide else 32 * j
            bst[to : to + 32, :] = hi
            bst[width + to : width + to + 32, :] = lo
    blank = [128 * j + 32 * shard for j in range(3) for shard in range(shards, 4)] if wide else [96]
    for to in blank:
        bst[to : to + 32, :] = jnp.zeros((32, AUX), bf16)
        bst[width + to : width + to + 32, :] = jnp.zeros((32, AUX), bf16)
    nt = (((1,), (1,)), ((), ()))

    def coulomb_step(k, carry):
        at = pl.ds(pl.multiple_of(k * DEPTH, DEPTH), DEPTH)
        both = lax.dot_general(ahi[:, at], bst[:, at], nt, preferred_element_type=f32)
        part = both[:, :width] + both[:, width:]
        part += lax.dot_general(alo[:, at], bst[:width, at], nt, preferred_element_type=f32)
        c_ref[...] += part
        return carry

    c_ref[...] = jnp.zeros_like(c_ref)
    lax.fori_loop(0, AUX // DEPTH, coulomb_step, 0)

    group = lax.broadcasted_iota(jnp.int32, (1, 128), 1) // 32
    square = lax.broadcasted_iota(jnp.int32, (32, 128), 0) == lax.broadcasted_iota(jnp.int32, (32, 128), 1)
    chosen = []
    for i in range(3):
        for j in range(3):
            count = jnp.int32(0)
            for n in range(6):
                count += ((pairs_ref[0, n] == i) & (pairs_ref[1, n] == j)).astype(jnp.int32)
            chosen.append(count.astype(f32))
    col = jnp.zeros((1, 128), f32)
    if wide:
        for shard in range(shards):
            col = jnp.where(group == shard, e_ref[col_at + shard : col_at + shard + 1, :], col)
    else:
        piece = e_ref[col_at : col_at + 1, :]
        for j in range(3):
            col = jnp.where(group == j, piece - oe_ref[j], col)
    for d in range(rows_total // 96):
        ea = jnp.sum(jnp.where(square, e_ref[row_at[d] : row_at[d] + 1, :], 0.0), axis=1, keepdims=True)
        for i in range(3):
            rows = slice(96 * d + 32 * i, 96 * d + 32 * i + 32)
            if wide:
                for j in range(3):
                    direct = c_ref[rows, 128 * j : 128 * j + 128]
                    other = c_ref[96 * d + 32 * j : 96 * d + 32 * j + 32, 128 * i : 128 * i + 128]
                    denominator = (oe_ref[i] + oe_ref[j]) - ea - col
                    hi, lo = split(chosen[3 * i + j] * ((2.0 * direct - other) / denominator))
                    whi[rows, 128 * j : 128 * j + 128] = hi
                    whi[rows, 384 + 128 * j : 512 + 128 * j] = hi
                    wlo[rows, 128 * j : 128 * j + 128] = lo
            else:
                direct = c_ref[rows, :]
                other = jnp.zeros((32, 128), f32)
                keep = jnp.zeros((1, 128), f32)
                for j in range(3):
                    moved = c_ref[96 * d + 32 * j : 96 * d + 32 * j + 32, :]
                    if j != i:
                        moved = pltpu.roll(moved, (32 * (j - i)) % 128, 1)
                    other = jnp.where(group == j, moved, other)
                    keep = jnp.where(group == j, chosen[3 * i + j], keep)
                denominator = oe_ref[i] - ea - col
                hi, lo = split(keep * ((2.0 * direct - other) / denominator))
                whi[rows, :128] = hi
                whi[rows, 128:] = hi
                wlo[rows, :] = lo

    for copy, _, _ in acc_copies:
        copy.wait()

    def out_copies(k):
        at = pl.ds(pl.multiple_of(k * 512, 512), 512)
        row = 0
        for n, out in enumerate(outs):
            h = out.shape[0]
            yield pltpu.make_async_copy(g_buf.at[row : row + h, at], out.at[:, at], out_sem.at[k, n])
            row += h

    def gamma_step(k, carry):
        at = pl.ds(pl.multiple_of(k * 512, 512), 512)
        g = jnp.dot(whi[...], bst[:, at], preferred_element_type=f32)
        g += jnp.dot(wlo[...], bst[:width, at], preferred_element_type=f32)
        if n_acc:
            g += g_buf[:, at]
        g_buf[:, at] = g
        for copy in out_copies(k):
            copy.start()
        return carry

    lax.fori_loop(0, AUX // 512, gamma_step, 0)
    for k in range(AUX // 512):
        for copy in out_copies(k):
            copy.wait()


def block(name, tables, a_list, row_at, b_list, col_at, acc_list, out_rows):
    a_list = list(a_list)
    b_list = list(b_list)
    smem = pl.BlockSpec(memory_space=pltpu.SMEM)
    vmem = pl.BlockSpec(memory_space=pltpu.VMEM)
    hbm = pl.BlockSpec(memory_space=pl.ANY)
    rows = sum(a.shape[0] for a in a_list)
    shards = sum(b.shape[0] for b in b_list) // 96
    width = 384 if shards > 1 else 128
    args = list(tables) + a_list + b_list + list(acc_list)
    counts = (len(a_list), len(b_list), len(acc_list), len(out_rows), shards, row_at, col_at)

    def body(*refs):
        block_kernel(*counts, *refs)

    dma = pltpu.SemaphoreType.DMA
    return pl.pallas_call(
        body,
        in_specs=[smem, smem, vmem] + [hbm] * (len(args) - 3),
        out_specs=[hbm] * len(out_rows),
        out_shape=[jax.ShapeDtypeStruct((n, AUX), f32) for n in out_rows],
        scratch_shapes=[
            pltpu.VMEM((rows, AUX), f32),
            pltpu.VMEM((96 * shards, AUX), f32),
            pltpu.VMEM((rows, AUX), f32),
            pltpu.VMEM((rows, AUX), bf16),
            pltpu.VMEM((rows, AUX), bf16),
            pltpu.VMEM((2 * width, AUX), bf16),
            pltpu.VMEM((rows, width), f32),
            pltpu.VMEM((rows, 2 * width), bf16),
            pltpu.VMEM((rows, width), bf16),
            dma((len(a_list),)),
            dma((len(b_list),)),
            dma((max(len(acc_list), 1),)),
            dma((AUX // 512, len(out_rows))),
        ],
        compiler_params=pltpu.CompilerParams(vmem_limit_bytes=36 * 1024 * 1024),
        cost_estimate=pl.CostEstimate(
            flops=2 * rows * width * AUX * 6, transcendentals=0, bytes_accessed=4 * AUX * (2 * rows + 96 * shards)
        ),
        name=name,
    )(*args)


def take_from(x, axis, step):
    n = lax.axis_size(axis)
    return lax.ppermute(x, axis, [(i, (i - step) % n) for i in range(n)])


def local(half_rows, screen, slot_shell, vir_coeff, occ_energy, vir_energy, pair_list):
    y = lax.axis_index("y")
    z = lax.axis_index("z")
    xh = lax.axis_index("xh")

    energy_row = jnp.tile(vir_energy, 4).reshape(1, 128)
    core = lax.axis_index("co")
    me = jnp.stack([lax.axis_index("xl") * 32 + y * 8 + z * 2 + xh, core]).astype(jnp.int32)
    rows = half_rows.reshape(2, 2, 96, AUX)
    given = lax.ppermute(gift(me, screen.T, rows), "co", [(0, 1), (1, 0)])
    meta = slot_map(me, slot_shell)
    most = meta[2, 0]

    def exchange(cap):
        def run(me, screen_t, meta, rows, given, energy_row, vir_coeff):
            packed = pack(cap, me, screen_t, meta, energy_row, rows, given)
            moved = lax.all_to_all(packed.reshape(64, -1, 128), ("xl",) + GROUP, 0, 0, tiled=True)
            chi, clo = coeff(vir_coeff)
            return transform(cap, me, meta, moved, chi, clo)

        return run

    level = (most > 5).astype(jnp.int32) + (most > 6).astype(jnp.int32)
    sent, energies = lax.switch(
        level, [exchange(5), exchange(6), exchange(8)], me, screen.T, meta, rows, given, energy_row, vir_coeff
    )
    received = lax.all_to_all(sent, GROUP, 0, 0, tiled=True)
    own = unpack(received)
    tables = (pair_list.T, occ_energy, energies)
    here, above, below, across = 0, 1, 2, 3

    y1 = take_from(own, "y", 1)
    y3 = take_from(own, "y", -1)
    z1 = take_from(own, "z", 1)
    z3 = take_from(own, "z", -1)
    x0 = take_from(own, "xh", 1)
    y1, y3, z1, z3, x0 = lax.optimization_barrier((y1, y3, z1, z3, x0))
    y2a = take_from(y1[:48], "y", 1)
    y2b = take_from(y3[48:], "y", -1)
    z2 = take_from(z3, "z", -1)
    x1 = take_from(x0, "z", 1)
    x3 = take_from(z3, "xh", 1)
    cols = [own, z1, z3, x0]
    rows, rows_at = [own, y1, y3, y2a, y2b], (here, above, below, across)
    own_acc, near_acc, far_acc = block("gamma_first", tables, rows, rows_at, cols, 4, [], [96, 192, 96])
    z2, x1, x3, own_acc, near_acc, far_acc = lax.optimization_barrier((z2, x1, x3, own_acc, near_acc, far_acc))
    x2a = take_from(z2[:32], "xh", 1)
    x2b = take_from(x1[32:64], "z", 1)
    x2c = take_from(x3[64:], "z", -1)
    own_acc, near_acc, far_acc = block(
        "gamma_next", tables, rows, rows_at, [z2, x1, x3], 8, [own_acc, near_acc, far_acc], [96, 192, 96]
    )
    tail = [x2a, x2b, x2c]
    g2a, g2b = block("gamma_far", tables, [y2a, y2b], (across,), tail, 11, [far_acc], [48, 48])
    up = take_from(g2a, "y", -1)
    down = take_from(g2b, "y", 1)
    g1a, g1b, g3a, g3b = block(
        "gamma_near", tables, [y1, y3], (above, below), tail, 11, [near_acc], [48, 48, 48, 48]
    )
    below_b = take_from(g1b, "y", -1)
    above_a = take_from(g3a, "y", 1)
    (g0,) = block("gamma_own", tables, [own], (here,), tail, 11, [own_acc], [96])
    below_a = take_from(g1a + up, "y", -1)
    above_b = take_from(g3b + down, "y", 1)
    from_below = jnp.concatenate([below_a, below_b], axis=0)
    from_above = jnp.concatenate([above_a, above_b], axis=0)
    return (g0 + from_below + from_above).reshape(3, 32, AUX)


def solution(mesh):
    wide = Mesh(mesh.devices.reshape(2, 2, 4, 4, 2), ALL)
    occ = ("xl", "co")
    in_specs = (P(None, ALL, None), P(None, ALL), P(), P(), P(occ), P(GROUP), P(occ, None))
    out_specs = P(occ, GROUP, None)
    return jax.shard_map(local, mesh=wide, in_specs=in_specs, out_specs=out_specs, check_vma=False)
```

profile of v0, /device:TPU:0, one launch (start us, length us, event | category | flops | bytes accessed | tf_op | source)
XLA Modules:
  0.0 251.9 jit_solution(6643460962406324934)
XLA Ops:
  0.1 3.3 %gift_rows.1 = f32[2,96,3072]{2,1,0:T(8,128)S(1)} custom-call(s32[2]{0:T(128)S(1)} %pad_add_fusion.me_ref, s32[4,12]{1,0:T(4,128)} %bitcast.26, f32[2,2,96,3072]{3,2,1,0:T(8,128)} %bitcast.19), custom_call_target="tpu_custom_call" | custom-call | tf_op jit(solution)/shard_map/gift_rows/pallas_call | solution.py:118
  8.1 97.2 %conditional.1 = ((f32[32,72,128]{2,1,0:T(8,128)}, f32[12,128]{1,0:T(8,128)S(1)})) conditional(s32[]{:T(128)} %bitcast.8, (s32[2]{0:T(128)S(1)}, s32[4,12]{1,0:T(4,128)S(1)}, s32[8,256]{1,0:T(8,128)S(1)}, f32[1,128]{1,0:T(1,128)S(1)}, f32[2,2,96,3072]{3,2,1,0:T(8,128)}, /*index=5*/f32[2,96,3072]{2,1,0:T(8,128)}, ...), branch_computations={%region_0.0_spmd, %region_1.0_spmd, %region_2.0_spmd} | conditional | bytes 33816672 | solution.py:580
  8.1 6.9 %pack_rows_8.1 = f32[2,32,152,128]{3,2,1,0:T(8,128)} custom-call(s32[2]{0:T(128)S(1)} %get-tuple-element.65.refs_0_, s32[4,12]{1,0:T(4,128)S(1)} %get-tuple-element.67.refs_1_, s32[8,256]{1,0:T(8,128)S(1)} %get-tuple-element.66.refs_2_.refs_1_, f32[1,128]{1,0:T(1,128)S(1)} %get-tuple-element.68.refs_3_, f32[2,2,96,3072]{3,2,1,0:T(8,128)} %get-tuple-element.69.refs_4_, ...), custom_call_target="tpu_custom_call" | custom-call | tf_op jit(solution)/shard_map/cond/branch_2_fun/pack_rows_8/pallas_call | solution.py:202
  15.0 11.8 %all-to-all-start.2 = ((f32[64,152,128]{2,1,0:T(8,128)}), f32[64,152,128]{2,1,0:T(8,128)}, u32[]{:S(2)}, u32[]{:S(2)}) async-start(f32[64,152,128]{2,1,0:T(8,128)} %bitcast.23), calls=%async_computation.2 | async-start | bytes 9961472 | tf_op jit(solution)/shard_map/cond/branch_2_fun/all_to_all | solution.py:573
  26.8 8.2 %split_coeff.5 = (bf16[1024,1152]{1,0:T(8,128)(2,1)}, bf16[1024,1152]{1,0:T(8,128)(2,1)}) custom-call(f32[1152,1024]{1,0:T(8,128)} %get-tuple-element.71.c_ref), custom_call_target="tpu_custom_call" | custom-call | tf_op jit(solution)/shard_map/cond/branch_2_fun/split_coeff/pallas_call | solution.py:226
  35.0 56.5 %all-to-all-done.2.refs_2_ = f32[64,152,128]{2,1,0:T(8,128)} async-done(((f32[64,152,128]{2,1,0:T(8,128)}), f32[64,152,128]{2,1,0:T(8,128)}, u32[]{:S(2)}, u32[]{:S(2)}) %all-to-all-start.2) | async-done | bytes 4980768 | tf_op jit(solution)/shard_map/cond/branch_2_fun/all_to_all | solution.py:573
  94.8 10.4 %transform_rows_8.1 = (f32[32,72,128]{2,1,0:T(8,128)}, f32[12,128]{1,0:T(8,128)S(1)}) custom-call(s32[2]{0:T(128)S(1)} %get-tuple-element.65.refs_0_, s32[8,256]{1,0:T(8,128)S(1)} %get-tuple-element.66.refs_2_.refs_1_, f32[64,152,128]{2,1,0:T(8,128)} %all-to-all-done.2.refs_2_, bf16[1024,1152]{1,0:T(8,128)(2,1)S(1)} %copy-done.4, ...), custom_call_target="tpu_custom_call" | custom-call | tf_op jit(solution)/shard_map/cond/branch_2_fun/transform_rows_8/pallas_call | solution.py:305
  105.4 24.4 %all_to_all.17.q_hbm = f32[32,72,128]{2,1,0:T(8,128)S(1)} all-to-all(f32[32,72,128]{2,1,0:T(8,128)} %get-tuple-element.100), channel_id=1, replica_groups=mesh['xl'=2,'co'=2,'y'=4,'z'=4,'xh'=2] {'y','z','xh'}, dimensions={0} | all-to-all | bytes 2359296 | tf_op jit(solution)/shard_map/all_to_all | solution.py:583
  129.8 3.0 %unpack_fitted.1.refs_3_.refs_8_ = f32[96,3072]{1,0:T(8,128)S(1)} custom-call(f32[32,72,128]{2,1,0:T(8,128)S(1)} %all_to_all.17.q_hbm), custom_call_target="tpu_custom_call" | custom-call | tf_op jit(solution)/shard_map/unpack_fitted/pallas_call | solution.py:362
  134.2 2.7 %collective-permute-start.3 = (f32[96,3072]{1,0:T(8,128)S(1)}, f32[96,3072]{1,0:T(8,128)S(1)}, u32[]{:S(2)}, u32[]{:S(2)}) collective-permute-start(f32[96,3072]{1,0:T(8,128)S(1)} %unpack_fitted.1.refs_3_.refs_8_), channel_id=1, source_target_pairs={{0,6},{2,0},{4,2},{6,4},{1,7},{3,1},{5,3},{7,5},{8,14},{10,8},{12,... | collective-permute-start | bytes 3538952 | tf_op jit(solution)/shard_map/ppermute | solution.py:554
  137.4 2.6 %collective-permute-start.1 = (f32[96,3072]{1,0:T(8,128)S(1)}, f32[96,3072]{1,0:T(8,128)S(1)}, u32[]{:S(2)}, u32[]{:S(2)}) collective-permute-start(f32[96,3072]{1,0:T(8,128)S(1)} %unpack_fitted.1.refs_3_.refs_8_), channel_id=1, source_target_pairs={{0,24},{8,0},{16,8},{24,16},{1,25},{9,1},{17,9},{25,17},{2,26},{10... | collective-permute-start | bytes 3538952 | tf_op jit(solution)/shard_map/ppermute | solution.py:554
  140.1 20.3 %collective-permute-done.5.refs_11_ = f32[96,3072]{1,0:T(8,128)S(1)} collective-permute-done((f32[96,3072]{1,0:T(8,128)S(1)}, f32[96,3072]{1,0:T(8,128)S(1)}, u32[]{:S(2)}, u32[]{:S(2)}) %collective-permute-start.5) | collective-permute-done | bytes 1179680 | tf_op jit(solution)/shard_map/ppermute | solution.py:554
  161.0 2.7 %collective-permute-done.2.refs_5_.refs_4_ = f32[96,3072]{1,0:T(8,128)S(1)} collective-permute-done((f32[96,3072]{1,0:T(8,128)S(1)}, f32[96,3072]{1,0:T(8,128)S(1)}, u32[]{:S(2)}, u32[]{:S(2)}) %collective-permute-start.2) | collective-permute-done | bytes 1179680 | tf_op jit(solution)/shard_map/ppermute | solution.py:554
  168.2 3.2 %collective-permute-start.9 = (f32[48,3072]{1,0:T(8,128)S(1)}, f32[48,3072]{1,0:T(8,128)S(1)}, u32[]{:S(2)}, u32[]{:S(2)}) collective-permute-start(f32[48,3072]{1,0:T(8,128)S(1)} %slice.19), channel_id=1, source_target_pairs={{0,24},{8,0},{16,8},{24,16},{1,25},{9,1},{17,9},{25,17},{2,26},{10... | collective-permute-start | bytes 1769480 | tf_op jit(solution)/shard_map/ppermute | solution.py:554
  171.5 8.8 %collective-permute-done.10.refs_7_.refs_4_ = f32[48,3072]{1,0:T(8,128)S(1)} collective-permute-done((f32[48,3072]{1,0:T(8,128)S(1)}, f32[48,3072]{1,0:T(8,128)S(1)}, u32[]{:S(2)}, u32[]{:S(2)}) %collective-permute-start.10) | collective-permute-done | bytes 589856 | tf_op jit(solution)/shard_map/ppermute | solution.py:554
  180.3 12.4 %gamma_first.1 = (f32[96,3072]{1,0:T(8,128)S(1)}, f32[192,3072]{1,0:T(8,128)S(1)}, f32[96,3072]{1,0:T(8,128)S(1)}) custom-call(s32[2,6]{1,0:T(2,128)S(1)} %bitcast.12, f32[3]{0:T(128)S(1)} %copy-done.8, f32[12,128]{1,0:T(8,128)S(1)} %get-tuple-element.99.refs_2_, f32[96,3072]{1,0:T(8,128)S(1)} %unpack_fitted.1.refs_3_.refs_8_, ...), custom_call_target="tpu_custom_call" | custom-call | flops 5435817984 | bytes 14155776 | tf_op jit(solution)/shard_map/gamma_first/pallas_call | solution.py:524
  196.6 12.7 %gamma_next.1 = (f32[96,3072]{1,0:T(8,128)S(1)}, f32[192,3072]{1,0:T(8,128)S(1)}, f32[96,3072]{1,0:T(8,128)S(1)}) custom-call(s32[2,6]{1,0:T(2,128)S(1)} %bitcast.13, f32[3]{0:T(128)S(1)} %copy-done.8, f32[12,128]{1,0:T(8,128)S(1)} %get-tuple-element.99.refs_2_, f32[96,3072]{1,0:T(8,128)S(1)} %unpack_fitted.1.refs_3_.refs_8_, ...), custom_call_target="tpu_custom_call" | custom-call | flops 5435817984 | bytes 12976128 | tf_op jit(solution)/shard_map/gamma_next/pallas_call | solution.py:524
  209.4 4.8 %gamma_far.1 = (f32[48,3072]{1,0:T(8,128)S(1)}, f32[48,3072]{1,0:T(8,128)S(1)}) custom-call(s32[2,6]{1,0:T(2,128)S(1)} %bitcast.14, f32[3]{0:T(128)S(1)} %copy-done.8, f32[12,128]{1,0:T(8,128)S(1)} %get-tuple-element.99.refs_2_, f32[48,3072]{1,0:T(8,128)S(1)} %collective-permute-done.9.refs_6_.refs_3_, ...), custom_call_target="tpu_custom_call" | custom-call | flops 452984832 | bytes 3538944 | tf_op jit(solution)/shard_map/gamma_far/pallas_call | solution.py:524
  217.5 5.9 %gamma_near.1 = (f32[48,3072]{1,0:T(8,128)S(1)}, f32[48,3072]{1,0:T(8,128)S(1)}, f32[48,3072]{1,0:T(8,128)S(1)}, f32[48,3072]{1,0:T(8,128)S(1)}) custom-call(s32[2,6]{1,0:T(2,128)S(1)} %bitcast.15, f32[3]{0:T(128)S(1)} %copy-done.8, f32[12,128]{1,0:T(8,128)S(1)} %get-tuple-element.99.refs_2_, f32[96,3072]{1,0:T(8,128)S(1)} %collective-permute-done.1.refs_4_.refs_3_, ...), custom_call_target="tpu_custom_call" | custom-call | flops 905969664 | bytes 5898240 | tf_op jit(solution)/shard_map/gamma_near/pallas_call | solution.py:524
  223.5 3.2 %collective-permute-start.17 = (f32[48,3072]{1,0:T(8,128)S(1)}, f32[48,3072]{1,0:T(8,128)S(1)}, u32[]{:S(2)}, u32[]{:S(2)}) collective-permute-start(f32[48,3072]{1,0:T(8,128)S(1)} %get-tuple-element.121), channel_id=1, source_target_pairs={{0,24},{8,0},{16,8},{24,16},{1,25},{9,1},{17,9},{25,17},{2,26},{10... | collective-permute-start | bytes 1769480 | tf_op jit(solution)/shard_map/ppermute | solution.py:554
  229.8 3.1 %collective-permute-start.19 = (f32[48,3072]{1,0:T(8,128)S(1)}, f32[48,3072]{1,0:T(8,128)S(1)}, u32[]{:S(2)}, u32[]{:S(2)}) collective-permute-start(f32[48,3072]{1,0:T(8,128)S(1)} %add.31), channel_id=1, source_target_pairs={{0,24},{8,0},{16,8},{24,16},{1,25},{9,1},{17,9},{25,17},{2,26},{10... | collective-permute-start | bytes 1769480 | tf_op jit(solution)/shard_map/ppermute | solution.py:554
  232.9 4.7 %gamma_own.1 = f32[96,3072]{1,0:T(8,128)S(1)} custom-call(s32[2,6]{1,0:T(2,128)S(1)} %bitcast.16, f32[3]{0:T(128)S(1)} %copy-done.8, f32[12,128]{1,0:T(8,128)S(1)} %get-tuple-element.99.refs_2_, f32[96,3072]{1,0:T(8,128)S(1)} %unpack_fitted.1.refs_3_.refs_8_, f32[32,3072]{1,0:T(8,128)S(1)} %collective-permute-done.11.refs_4_.refs_5_, ...), custom_call_target="tpu_custom_call" | custom-call | flops 452984832 | bytes 3538944 | tf_op jit(solution)/shard_map/gamma_own/pallas_call | solution.py:524
  237.5 4.4 %collective-permute-done.16 = f32[48,3072]{1,0:T(8,128)S(1)} collective-permute-done((f32[48,3072]{1,0:T(8,128)S(1)}, f32[48,3072]{1,0:T(8,128)S(1)}, u32[]{:S(2)}, u32[]{:S(2)}) %collective-permute-start.16) | collective-permute-done | bytes 589856 | tf_op jit(solution)/shard_map/ppermute | solution.py:554
  242.2 8.4 %collective-permute-done.15 = f32[48,3072]{1,0:T(8,128)S(1)} collective-permute-done((f32[48,3072]{1,0:T(8,128)S(1)}, f32[48,3072]{1,0:T(8,128)S(1)}, u32[]{:S(2)}, u32[]{:S(2)}) %collective-permute-start.15) | collective-permute-done | bytes 589856 | tf_op jit(solution)/shard_map/ppermute | solution.py:554
  (58 shorter events, 25.7 us)
Async XLA Ops:
  0.1 8.0 %copy-start.9 = (s32[12,4]{0,1:T(4,128)S(1)}, s32[12,4]{0,1:T(4,128)}, u32[]{:S(2)}) copy-start(s32[12,4]{0,1:T(4,128)} %param.11) | copy-start | bytes 580
  3.4 4.7 %collective-permute-start = (f32[2,96,3072]{2,1,0:T(8,128)S(1)}, f32[2,96,3072]{2,1,0:T(8,128)}, u32[]{:S(2)}, u32[]{:S(2)}) collective-permute-start(f32[2,96,3072]{2,1,0:T(8,128)S(1)} %gift_rows.1), channel_id=1, source_target_pairs={{0,32},{32,0},{1,33},{33,1},{2,34},{34,2},{3,35},{35,3},{4,36},{36... | collective-permute-start | bytes 7077896 | tf_op jit(solution)/shard_map/ppermute | solution.py:566
  15.0 76.4 %all-to-all-start.2 = ((f32[64,152,128]{2,1,0:T(8,128)}), f32[64,152,128]{2,1,0:T(8,128)}, u32[]{:S(2)}, u32[]{:S(2)}) async-start(f32[64,152,128]{2,1,0:T(8,128)} %bitcast.23), calls=%async_computation.2 | async-start | bytes 9961472 | tf_op jit(solution)/shard_map/cond/branch_2_fun/all_to_all | solution.py:573
  132.8 47.5 %copy-start.6 = (s32[6,2]{0,1:T(2,128)S(1)}, s32[6,2]{0,1:T(2,128)}, u32[]{:S(2)}) copy-start(s32[6,2]{0,1:T(2,128)} %param.16) | copy-start | bytes 148
  132.8 47.5 %copy-start.8 = (f32[3]{0:T(128)S(1)}, f32[3]{0:T(128)}, u32[]{:S(2)}) copy-start(f32[3]{0:T(128)} %refs_1_.9) | copy-start | bytes 40
  132.8 27.6 %collective-permute-start.5 = (f32[96,3072]{1,0:T(8,128)S(1)}, f32[96,3072]{1,0:T(8,128)S(1)}, u32[]{:S(2)}, u32[]{:S(2)}) collective-permute-start(f32[96,3072]{1,0:T(8,128)S(1)} %unpack_fitted.1.refs_3_.refs_8_), channel_id=1, source_target_pairs={{0,1},{1,0},{2,3},{3,2},{4,5},{5,4},{6,7},{7,6},{8,9},{9,8},{10,11... | collective-permute-start | bytes 3538952 | tf_op jit(solution)/shard_map/ppermute | solution.py:554
  133.6 27.4 %collective-permute-start.4 = (f32[96,3072]{1,0:T(8,128)S(1)}, f32[96,3072]{1,0:T(8,128)S(1)}, u32[]{:S(2)}, u32[]{:S(2)}) collective-permute-start(f32[96,3072]{1,0:T(8,128)S(1)} %unpack_fitted.1.refs_3_.refs_8_), channel_id=1, source_target_pairs={{0,2},{2,4},{4,6},{6,0},{1,3},{3,5},{5,7},{7,1},{8,10},{10,12},{12... | collective-permute-start | bytes 3538952 | tf_op jit(solution)/shard_map/ppermute | solution.py:554
  134.2 26.9 %collective-permute-start.3 = (f32[96,3072]{1,0:T(8,128)S(1)}, f32[96,3072]{1,0:T(8,128)S(1)}, u32[]{:S(2)}, u32[]{:S(2)}) collective-permute-start(f32[96,3072]{1,0:T(8,128)S(1)} %unpack_fitted.1.refs_3_.refs_8_), channel_id=1, source_target_pairs={{0,6},{2,0},{4,2},{6,4},{1,7},{3,1},{5,3},{7,5},{8,14},{10,8},{12,... | collective-permute-start | bytes 3538952 | tf_op jit(solution)/shard_map/ppermute | solution.py:554
  136.8 26.9 %collective-permute-start.2 = (f32[96,3072]{1,0:T(8,128)S(1)}, f32[96,3072]{1,0:T(8,128)S(1)}, u32[]{:S(2)}, u32[]{:S(2)}) collective-permute-start(f32[96,3072]{1,0:T(8,128)S(1)} %unpack_fitted.1.refs_3_.refs_8_), channel_id=1, source_target_pairs={{0,8},{8,16},{16,24},{24,0},{1,9},{9,17},{17,25},{25,1},{2,10},{10... | collective-permute-start | bytes 3538952 | tf_op jit(solution)/shard_map/ppermute | solution.py:554
  137.4 26.3 %collective-permute-start.1 = (f32[96,3072]{1,0:T(8,128)S(1)}, f32[96,3072]{1,0:T(8,128)S(1)}, u32[]{:S(2)}, u32[]{:S(2)}) collective-permute-start(f32[96,3072]{1,0:T(8,128)S(1)} %unpack_fitted.1.refs_3_.refs_8_), channel_id=1, source_target_pairs={{0,24},{8,0},{16,8},{24,16},{1,25},{9,1},{17,9},{25,17},{2,26},{10... | collective-permute-start | bytes 3538952 | tf_op jit(solution)/shard_map/ppermute | solution.py:554
  163.7 28.9 %collective-permute-start.7 = (f32[96,3072]{1,0:T(8,128)S(1)}, f32[96,3072]{1,0:T(8,128)S(1)}, u32[]{:S(2)}, u32[]{:S(2)}) collective-permute-start(f32[96,3072]{1,0:T(8,128)S(1)} %collective-permute-done.5.refs_11_), channel_id=1, source_target_pairs={{0,6},{2,0},{4,2},{6,4},{1,7},{3,1},{5,3},{7,5},{8,14},{10,8},{12,... | collective-permute-start | bytes 3538952 | tf_op jit(solution)/shard_map/ppermute | solution.py:554
  164.0 28.7 %collective-permute-start.8 = (f32[96,3072]{1,0:T(8,128)S(1)}, f32[96,3072]{1,0:T(8,128)S(1)}, u32[]{:S(2)}, u32[]{:S(2)}) collective-permute-start(f32[96,3072]{1,0:T(8,128)S(1)} %collective-permute-done.4.refs_10_), channel_id=1, source_target_pairs={{0,1},{1,0},{2,3},{3,2},{4,5},{5,4},{6,7},{7,6},{8,9},{9,8},{10,11... | collective-permute-start | bytes 3538952 | tf_op jit(solution)/shard_map/ppermute | solution.py:554
  166.3 26.3 %collective-permute-start.6 = (f32[96,3072]{1,0:T(8,128)S(1)}, f32[96,3072]{1,0:T(8,128)S(1)}, u32[]{:S(2)}, u32[]{:S(2)}) collective-permute-start(f32[96,3072]{1,0:T(8,128)S(1)} %collective-permute-done.4.refs_10_), channel_id=1, source_target_pairs={{0,2},{2,4},{4,6},{6,0},{1,3},{3,5},{5,7},{7,1},{8,10},{10,12},{12... | collective-permute-start | bytes 3538952 | tf_op jit(solution)/shard_map/ppermute | solution.py:554
  168.2 12.1 %collective-permute-start.10 = (f32[48,3072]{1,0:T(8,128)S(1)}, f32[48,3072]{1,0:T(8,128)S(1)}, u32[]{:S(2)}, u32[]{:S(2)}) collective-permute-start(f32[48,3072]{1,0:T(8,128)S(1)} %slice.20), channel_id=1, source_target_pairs={{0,8},{8,16},{16,24},{24,0},{1,9},{9,17},{17,25},{25,1},{2,10},{10... | collective-permute-start | bytes 1769480 | tf_op jit(solution)/shard_map/ppermute | solution.py:554
  168.2 12.0 %collective-permute-start.9 = (f32[48,3072]{1,0:T(8,128)S(1)}, f32[48,3072]{1,0:T(8,128)S(1)}, u32[]{:S(2)}, u32[]{:S(2)}) collective-permute-start(f32[48,3072]{1,0:T(8,128)S(1)} %slice.19), channel_id=1, source_target_pairs={{0,24},{8,0},{16,8},{24,16},{1,25},{9,1},{17,9},{25,17},{2,26},{10... | collective-permute-start | bytes 1769480 | tf_op jit(solution)/shard_map/ppermute | solution.py:554
  192.8 16.5 %collective-permute-start.11 = (f32[32,3072]{1,0:T(8,128)S(1)}, f32[32,3072]{1,0:T(8,128)S(1)}, u32[]{:S(2)}, u32[]{:S(2)}) collective-permute-start(f32[32,3072]{1,0:T(8,128)S(1)} %slice.21), channel_id=1, source_target_pairs={{0,1},{1,0},{2,3},{3,2},{4,5},{5,4},{6,7},{7,6},{8,9},{9,8},{10,11... | collective-permute-start | bytes 1179656 | tf_op jit(solution)/shard_map/ppermute | solution.py:554
  194.6 14.8 %collective-permute-start.12 = (f32[32,3072]{1,0:T(8,128)S(1)}, f32[32,3072]{1,0:T(8,128)S(1)}, u32[]{:S(2)}, u32[]{:S(2)}) collective-permute-start(f32[32,3072]{1,0:T(8,128)S(1)} %slice.22), channel_id=1, source_target_pairs={{0,6},{2,0},{4,2},{6,4},{1,7},{3,1},{5,3},{7,5},{8,14},{10,8},{12,... | collective-permute-start | bytes 1179656 | tf_op jit(solution)/shard_map/ppermute | solution.py:554
  196.3 13.0 %collective-permute-start.13 = (f32[32,3072]{1,0:T(8,128)S(1)}, f32[32,3072]{1,0:T(8,128)S(1)}, u32[]{:S(2)}, u32[]{:S(2)}) collective-permute-start(f32[32,3072]{1,0:T(8,128)S(1)} %slice.23), channel_id=1, source_target_pairs={{0,2},{2,4},{4,6},{6,0},{1,3},{3,5},{5,7},{7,1},{8,10},{10,12},{12... | collective-permute-start | bytes 1179656 | tf_op jit(solution)/shard_map/ppermute | solution.py:554
  214.2 15.2 %collective-permute-start.14 = (f32[48,3072]{1,0:T(8,128)S(1)}, f32[48,3072]{1,0:T(8,128)S(1)}, u32[]{:S(2)}, u32[]{:S(2)}) collective-permute-start(f32[48,3072]{1,0:T(8,128)S(1)} %get-tuple-element.119), channel_id=1, source_target_pairs={{0,8},{8,16},{16,24},{24,0},{1,9},{9,17},{17,25},{25,1},{2,10},{10... | collective-permute-start | bytes 1769480 | tf_op jit(solution)/shard_map/ppermute | solution.py:554
  215.1 14.6 %collective-permute-start.18 = (f32[48,3072]{1,0:T(8,128)S(1)}, f32[48,3072]{1,0:T(8,128)S(1)}, u32[]{:S(2)}, u32[]{:S(2)}) collective-permute-start(f32[48,3072]{1,0:T(8,128)S(1)} %get-tuple-element.123), channel_id=1, source_target_pairs={{0,24},{8,0},{16,8},{24,16},{1,25},{9,1},{17,9},{25,17},{2,26},{10... | collective-permute-start | bytes 1769480 | tf_op jit(solution)/shard_map/ppermute | solution.py:554
  223.4 18.5 %collective-permute-start.16 = (f32[48,3072]{1,0:T(8,128)S(1)}, f32[48,3072]{1,0:T(8,128)S(1)}, u32[]{:S(2)}, u32[]{:S(2)}) collective-permute-start(f32[48,3072]{1,0:T(8,128)S(1)} %get-tuple-element.120), channel_id=1, source_target_pairs={{0,8},{8,16},{16,24},{24,0},{1,9},{9,17},{17,25},{25,1},{2,10},{10... | collective-permute-start | bytes 1769480 | tf_op jit(solution)/shard_map/ppermute | solution.py:554
  223.5 18.7 %collective-permute-start.17 = (f32[48,3072]{1,0:T(8,128)S(1)}, f32[48,3072]{1,0:T(8,128)S(1)}, u32[]{:S(2)}, u32[]{:S(2)}) collective-permute-start(f32[48,3072]{1,0:T(8,128)S(1)} %get-tuple-element.121), channel_id=1, source_target_pairs={{0,24},{8,0},{16,8},{24,16},{1,25},{9,1},{17,9},{25,17},{2,26},{10... | collective-permute-start | bytes 1769480 | tf_op jit(solution)/shard_map/ppermute | solution.py:554
  229.4 21.3 %collective-permute-start.15 = (f32[48,3072]{1,0:T(8,128)S(1)}, f32[48,3072]{1,0:T(8,128)S(1)}, u32[]{:S(2)}, u32[]{:S(2)}) collective-permute-start(f32[48,3072]{1,0:T(8,128)S(1)} %add.29), channel_id=1, source_target_pairs={{0,8},{8,16},{16,24},{24,0},{1,9},{9,17},{17,25},{25,1},{2,10},{10... | collective-permute-start | bytes 1769480 | tf_op jit(solution)/shard_map/ppermute | solution.py:554
  229.8 20.9 %collective-permute-start.19 = (f32[48,3072]{1,0:T(8,128)S(1)}, f32[48,3072]{1,0:T(8,128)S(1)}, u32[]{:S(2)}, u32[]{:S(2)}) collective-permute-start(f32[48,3072]{1,0:T(8,128)S(1)} %add.31), channel_id=1, source_target_pairs={{0,24},{8,0},{16,8},{24,16},{1,25},{9,1},{17,9},{25,17},{2,26},{10... | collective-permute-start | bytes 1769480 | tf_op jit(solution)/shard_map/ppermute | solution.py:554
  (4 other events, 10.2 us)
where the time goes:
time: 252 us
  waiting for transfers between devices  106 us (42%)
  Pallas kernels  73.5 us (29%)
  starting transfers between devices  40.6 us (16%)
  blocking collectives  24.4 us (10%)
  local copies, waits for them, and re-layouts  4.26 us (2%)
    all_to_all x1, waiting for transfers between devices, run(): lax.all_to_all(packed.reshape(64, -1, 128), ('xl',) + GROUP, 0, 0, tiled=...  56.5 us
    ppermute x19, waiting for transfers between devices, take_from(): return lax.ppermute(x, axis, [(i, (i - step) % n) for i in range(n)])  48.2 us
    pallas_call x5, Pallas kernels, block(): pl.pallas_call(body, in_specs=[smem, smem, vmem] + [hbm] * (len(args) - 3...  40.5 us
    ppermute x19, starting transfers between devices, take_from(): return lax.ppermute(x, axis, [(i, (i - step) % n) for i in range(n)])  28.7 us
    all_to_all x1, blocking collectives, local(): received = lax.all_to_all(sent, GROUP, 0, 0, tiled=True)  24.4 us
    all_to_all x1, starting transfers between devices, run(): lax.all_to_all(packed.reshape(64, -1, 128), ('xl',) + GROUP, 0, 0, tiled=...  11.8 us
    pallas_call x1, Pallas kernels, transform(): pl.pallas_call(body, grid=(2,), in_specs=[pl.BlockSpec(memory_space=pltpu...  10.4 us
    pallas_call x1, Pallas kernels, coeff(): pl.pallas_call(coeff_kernel, grid=(9,), in_specs=[pl.BlockSpec((128, NVIR...  8.18 us
  transfers between devices with their start and end apart: 21, of which 10 were waited for; matrix products, arithmetic and copies ran while one was open for 0% of the time, Pallas kernels for 18%

commit v1 on v0

--- a/solution.py
+++ b/solution.py
@@ -229,7 +229,7 @@
         in_specs=[pl.BlockSpec((128, NVIR), lambda k: (k, 0))],
         out_specs=[pl.BlockSpec((NVIR, 128), lambda k: (0, k))] * 2,
         out_shape=[jax.ShapeDtypeStruct((NVIR, ROWS), bf16)] * 2,
-        compiler_params=params(),
+        compiler_params=pltpu.CompilerParams(vmem_limit_bytes=64500 * 1024),
         name="split_coeff",
     )(vir_coeff)
 
@@ -240,7 +240,16 @@
 )
 
 
-def transform_kernel(cap, me_ref, map_ref, r_hbm, chi_ref, clo_ref, o_ref, e_ref, r_ref, xs, sem):
+def transform_kernel(cap, me_ref, map_ref, r_hbm, hi_hbm, lo_hbm, o_ref, e_ref, r_ref, chi_ref, clo_ref, xs, sem, c_sem):
+    step = pl.program_id(0)
+
+    def halves(m):
+        at = pl.ds(pl.multiple_of(512 * m, 512), 512)
+        return (
+            pltpu.make_async_copy(hi_hbm.at[at], chi_ref.at[at], c_sem.at[0, m]),
+            pltpu.make_async_copy(lo_hbm.at[at], clo_ref.at[at], c_sem.at[1, m]),
+        )
+
     @pl.when(pl.program_id(0) == 0)
     def _():
         copies = [
@@ -249,6 +258,9 @@
         ]
         for copy in copies:
             copy.start()
+        for m in range(2):
+            for copy in halves(m):
+                copy.start()
         for copy in copies:
             copy.wait()
         blk = me_ref[0] % 32
@@ -281,9 +293,12 @@
 
         lax.fori_loop(0, NSH // 2, body, 0, unroll=4)
 
-    both = jnp.dot(chi_ref[...], xs[...], preferred_element_type=f32)
+    for copy in halves(step):
+        copy.wait()
+    mine = pl.ds(pl.multiple_of(512 * step, 512), 512)
+    both = jnp.dot(chi_ref[mine, :], xs[...], preferred_element_type=f32)
     y = both[:, :384] + both[:, 384:]
-    y += jnp.dot(clo_ref[...], xs[:, :384], preferred_element_type=f32)
+    y += jnp.dot(clo_ref[mine, :], xs[:, :384], preferred_element_type=f32)
     lane = lax.broadcasted_iota(jnp.int32, (8, 128), 1) // 32
     for k in range(16):
         last = jnp.zeros((8, 128), f32)
@@ -309,17 +324,20 @@
             pl.BlockSpec(memory_space=pltpu.SMEM),
             pl.BlockSpec(memory_space=pltpu.SMEM),
             pl.BlockSpec(memory_space=pl.ANY),
-            pl.BlockSpec((512, ROWS), lambda m: (m, 0)),
-            pl.BlockSpec((512, ROWS), lambda m: (m, 0)),
+            pl.BlockSpec(memory_space=pl.ANY),
+            pl.BlockSpec(memory_space=pl.ANY),
         ],
         out_specs=[pl.BlockSpec((16, 72, 128), lambda m: (m, 0, 0)), pl.BlockSpec((12, 128), lambda m: (0, 0))],
         out_shape=[jax.ShapeDtypeStruct((32, 72, 128), f32), jax.ShapeDtypeStruct((12, 128), f32)],
         scratch_shapes=[
             pltpu.VMEM((64, message_rows(cap), 128), f32),
+            pltpu.VMEM((NVIR, ROWS), bf16),
+            pltpu.VMEM((NVIR, ROWS), bf16),
             pltpu.VMEM((ROWS, 768), bf16),
             pltpu.SemaphoreType.DMA((4,)),
+            pltpu.SemaphoreType.DMA((2, 2)),
         ],
-        compiler_params=pltpu.CompilerParams(vmem_limit_bytes=36 * 1024 * 1024),
+        compiler_params=pltpu.CompilerParams(vmem_limit_bytes=60 * 1024 * 1024),
         name=f"transform_rows_{cap}",
     )(me, meta, rows, chi, clo)
 

time: 252 us -> 249 us (0.988)
  local copies, waits for them, and re-layouts: 4.26 us -> 0.93 us
    cond x4 -> x0, local copies, waits for them, and re-layouts: 3.33 us -> none
where the time goes in v1:
time: 249 us
  waiting for transfers between devices  106 us (43%)
  Pallas kernels  73.7 us (30%)
  starting transfers between devices  40.6 us (16%)
  blocking collectives  24.2 us (10%)
    all_to_all x1, waiting for transfers between devices, run(): lax.all_to_all(packed.reshape(64, -1, 128), ('xl',) + GROUP, 0, 0, tiled=...  56.5 us
    ppermute x19, waiting for transfers between devices, take_from(): return lax.ppermute(x, axis, [(i, (i - step) % n) for i in range(n)])  48.6 us
    pallas_call x5, Pallas kernels, block(): pl.pallas_call(body, in_specs=[smem, smem, vmem] + [hbm] * (len(args) - 3...  40.5 us
    ppermute x19, starting transfers between devices, take_from(): return lax.ppermute(x, axis, [(i, (i - step) % n) for i in range(n)])  28.7 us
    all_to_all x1, blocking collectives, local(): received = lax.all_to_all(sent, GROUP, 0, 0, tiled=True)  24.2 us
    all_to_all x1, starting transfers between devices, run(): lax.all_to_all(packed.reshape(64, -1, 128), ('xl',) + GROUP, 0, 0, tiled=...  11.8 us
    pallas_call x1, Pallas kernels, transform(): pl.pallas_call(body, grid=(2,), in_specs=[pl.BlockSpec(memory_space=pltpu...  10.7 us
    pallas_call x1, Pallas kernels, coeff(): pl.pallas_call(coeff_kernel, grid=(9,), in_specs=[pl.BlockSpec((128, NVIR...  8.16 us
  transfers between devices with their start and end apart: 21, of which 10 were waited for; matrix products, arithmetic and copies ran while one was open for 0% of the time, Pallas kernels for 18%

profile of v1, /device:TPU:0, one launch (start us, length us, event | category | flops | bytes accessed | tf_op | source)
XLA Modules:
  0.0 248.9 jit_solution(7799273504814541236)
XLA Ops:
  0.1 3.3 %gift_rows.1 = f32[2,96,3072]{2,1,0:T(8,128)S(1)} custom-call(s32[2]{0:T(128)S(1)} %pad_add_fusion.me_ref, s32[4,12]{1,0:T(4,128)} %bitcast.26, f32[2,2,96,3072]{3,2,1,0:T(8,128)} %bitcast.19), custom_call_target="tpu_custom_call" | custom-call | tf_op jit(solution)/shard_map/gift_rows/pallas_call | solution.py:118
  8.1 94.2 %conditional.1 = ((f32[32,72,128]{2,1,0:T(8,128)S(1)}, f32[12,128]{1,0:T(8,128)S(1)})) conditional(s32[]{:T(128)} %bitcast.8, (s32[2]{0:T(128)S(1)}, s32[4,12]{1,0:T(4,128)S(1)}, s32[8,256]{1,0:T(8,128)S(1)}, f32[1,128]{1,0:T(1,128)S(1)}, f32[2,2,96,3072]{3,2,1,0:T(8,128)}, /*index=5*/f32[2,96,3072]{2,1,0:T(8,128)}, ...), branch_computations={%region_0.0_spmd, %region_1.0_spmd, %region_2.0_spmd} | conditional | bytes 14942248 | solution.py:598
  8.1 6.9 %pack_rows_8.1 = f32[2,32,152,128]{3,2,1,0:T(8,128)} custom-call(s32[2]{0:T(128)S(1)} %get-tuple-element.65.refs_0_, s32[4,12]{1,0:T(4,128)S(1)} %get-tuple-element.67.refs_1_, s32[8,256]{1,0:T(8,128)S(1)} %get-tuple-element.66.refs_2_.refs_1_, f32[1,128]{1,0:T(1,128)S(1)} %get-tuple-element.68.refs_3_, f32[2,2,96,3072]{3,2,1,0:T(8,128)} %get-tuple-element.69.refs_4_, ...), custom_call_target="tpu_custom_call" | custom-call | tf_op jit(solution)/shard_map/cond/branch_2_fun/pack_rows_8/pallas_call | solution.py:202
  15.0 11.8 %all-to-all-start.2 = ((f32[64,152,128]{2,1,0:T(8,128)}), f32[64,152,128]{2,1,0:T(8,128)}, u32[]{:S(2)}, u32[]{:S(2)}) async-start(f32[64,152,128]{2,1,0:T(8,128)} %bitcast.23), calls=%async_computation.2 | async-start | bytes 9961472 | tf_op jit(solution)/shard_map/cond/branch_2_fun/all_to_all | solution.py:591
  26.8 8.2 %split_coeff.5 = (bf16[1024,1152]{1,0:T(8,128)(2,1)}, bf16[1024,1152]{1,0:T(8,128)(2,1)}) custom-call(f32[1152,1024]{1,0:T(8,128)} %get-tuple-element.71.c_ref), custom_call_target="tpu_custom_call" | custom-call | tf_op jit(solution)/shard_map/cond/branch_2_fun/split_coeff/pallas_call | solution.py:226
  34.9 56.5 %all-to-all-done.2.refs_2_ = f32[64,152,128]{2,1,0:T(8,128)} async-done(((f32[64,152,128]{2,1,0:T(8,128)}), f32[64,152,128]{2,1,0:T(8,128)}, u32[]{:S(2)}, u32[]{:S(2)}) %all-to-all-start.2) | async-done | bytes 4980768 | tf_op jit(solution)/shard_map/cond/branch_2_fun/all_to_all | solution.py:591
  91.4 10.7 %transform_rows_8.1 = (f32[32,72,128]{2,1,0:T(8,128)S(1)}, f32[12,128]{1,0:T(8,128)S(1)}) custom-call(s32[2]{0:T(128)S(1)} %get-tuple-element.65.refs_0_, s32[8,256]{1,0:T(8,128)S(1)} %get-tuple-element.66.refs_2_.refs_1_, f32[64,152,128]{2,1,0:T(8,128)} %all-to-all-done.2.refs_2_, bf16[1024,1152]{1,0:T(8,128)(2,1)} %get-tuple-element.72.refs_3_, ...), custom_call_target="tpu_custom_call" | custom-call | tf_op jit(solution)/shard_map/cond/branch_2_fun/transform_rows_8/pallas_call | solution.py:320
  102.3 24.2 %all_to_all.17.q_hbm = f32[32,72,128]{2,1,0:T(8,128)S(1)} all-to-all(f32[32,72,128]{2,1,0:T(8,128)S(1)} %get-tuple-element.100), channel_id=1, replica_groups=mesh['xl'=2,'co'=2,'y'=4,'z'=4,'xh'=2] {'y','z','xh'}, dimensions={0} | all-to-all | bytes 2359296 | tf_op jit(solution)/shard_map/all_to_all | solution.py:601
  126.5 3.0 %unpack_fitted.1.refs_3_.refs_8_ = f32[96,3072]{1,0:T(8,128)S(1)} custom-call(f32[32,72,128]{2,1,0:T(8,128)S(1)} %all_to_all.17.q_hbm), custom_call_target="tpu_custom_call" | custom-call | tf_op jit(solution)/shard_map/unpack_fitted/pallas_call | solution.py:380
  130.9 2.7 %collective-permute-start.3 = (f32[96,3072]{1,0:T(8,128)S(1)}, f32[96,3072]{1,0:T(8,128)S(1)}, u32[]{:S(2)}, u32[]{:S(2)}) collective-permute-start(f32[96,3072]{1,0:T(8,128)S(1)} %unpack_fitted.1.refs_3_.refs_8_), channel_id=1, source_target_pairs={{0,6},{2,0},{4,2},{6,4},{1,7},{3,1},{5,3},{7,5},{8,14},{10,8},{12,... | collective-permute-start | bytes 3538952 | tf_op jit(solution)/shard_map/ppermute | solution.py:572
  136.8 20.4 %collective-permute-done.5.refs_11_ = f32[96,3072]{1,0:T(8,128)S(1)} collective-permute-done((f32[96,3072]{1,0:T(8,128)S(1)}, f32[96,3072]{1,0:T(8,128)S(1)}, u32[]{:S(2)}, u32[]{:S(2)}) %collective-permute-start.5) | collective-permute-done | bytes 1179680 | tf_op jit(solution)/shard_map/ppermute | solution.py:572
  157.9 2.7 %collective-permute-done.2.refs_5_.refs_4_ = f32[96,3072]{1,0:T(8,128)S(1)} collective-permute-done((f32[96,3072]{1,0:T(8,128)S(1)}, f32[96,3072]{1,0:T(8,128)S(1)}, u32[]{:S(2)}, u32[]{:S(2)}) %collective-permute-start.2) | collective-permute-done | bytes 1179680 | tf_op jit(solution)/shard_map/ppermute | solution.py:572
  165.1 3.2 %collective-permute-start.9 = (f32[48,3072]{1,0:T(8,128)S(1)}, f32[48,3072]{1,0:T(8,128)S(1)}, u32[]{:S(2)}, u32[]{:S(2)}) collective-permute-start(f32[48,3072]{1,0:T(8,128)S(1)} %slice.19), channel_id=1, source_target_pairs={{0,24},{8,0},{16,8},{24,16},{1,25},{9,1},{17,9},{25,17},{2,26},{10... | collective-permute-start | bytes 1769480 | tf_op jit(solution)/shard_map/ppermute | solution.py:572
  168.3 8.9 %collective-permute-done.10.refs_7_.refs_4_ = f32[48,3072]{1,0:T(8,128)S(1)} collective-permute-done((f32[48,3072]{1,0:T(8,128)S(1)}, f32[48,3072]{1,0:T(8,128)S(1)}, u32[]{:S(2)}, u32[]{:S(2)}) %collective-permute-start.10) | collective-permute-done | bytes 589856 | tf_op jit(solution)/shard_map/ppermute | solution.py:572
  177.2 12.4 %gamma_first.1 = (f32[96,3072]{1,0:T(8,128)S(1)}, f32[192,3072]{1,0:T(8,128)S(1)}, f32[96,3072]{1,0:T(8,128)S(1)}) custom-call(s32[2,6]{1,0:T(2,128)S(1)} %bitcast.12, f32[3]{0:T(128)S(1)} %copy-done.2, f32[12,128]{1,0:T(8,128)S(1)} %get-tuple-element.99.refs_2_, f32[96,3072]{1,0:T(8,128)S(1)} %unpack_fitted.1.refs_3_.refs_8_, ...), custom_call_target="tpu_custom_call" | custom-call | flops 5435817984 | bytes 14155776 | tf_op jit(solution)/shard_map/gamma_first/pallas_call | solution.py:542
  193.6 12.7 %gamma_next.1 = (f32[96,3072]{1,0:T(8,128)S(1)}, f32[192,3072]{1,0:T(8,128)S(1)}, f32[96,3072]{1,0:T(8,128)S(1)}) custom-call(s32[2,6]{1,0:T(2,128)S(1)} %bitcast.13, f32[3]{0:T(128)S(1)} %copy-done.2, f32[12,128]{1,0:T(8,128)S(1)} %get-tuple-element.99.refs_2_, f32[96,3072]{1,0:T(8,128)S(1)} %unpack_fitted.1.refs_3_.refs_8_, ...), custom_call_target="tpu_custom_call" | custom-call | flops 5435817984 | bytes 12976128 | tf_op jit(solution)/shard_map/gamma_next/pallas_call | solution.py:542
  206.3 4.8 %gamma_far.1 = (f32[48,3072]{1,0:T(8,128)S(1)}, f32[48,3072]{1,0:T(8,128)S(1)}) custom-call(s32[2,6]{1,0:T(2,128)S(1)} %bitcast.14, f32[3]{0:T(128)S(1)} %copy-done.2, f32[12,128]{1,0:T(8,128)S(1)} %get-tuple-element.99.refs_2_, f32[48,3072]{1,0:T(8,128)S(1)} %collective-permute-done.9.refs_6_.refs_3_, ...), custom_call_target="tpu_custom_call" | custom-call | flops 452984832 | bytes 3538944 | tf_op jit(solution)/shard_map/gamma_far/pallas_call | solution.py:542
  214.4 5.9 %gamma_near.1 = (f32[48,3072]{1,0:T(8,128)S(1)}, f32[48,3072]{1,0:T(8,128)S(1)}, f32[48,3072]{1,0:T(8,128)S(1)}, f32[48,3072]{1,0:T(8,128)S(1)}) custom-call(s32[2,6]{1,0:T(2,128)S(1)} %bitcast.15, f32[3]{0:T(128)S(1)} %copy-done.2, f32[12,128]{1,0:T(8,128)S(1)} %get-tuple-element.99.refs_2_, f32[96,3072]{1,0:T(8,128)S(1)} %collective-permute-done.1.refs_4_.refs_3_, ...), custom_call_target="tpu_custom_call" | custom-call | flops 905969664 | bytes 5898240 | tf_op jit(solution)/shard_map/gamma_near/pallas_call | solution.py:542
  220.5 3.2 %collective-permute-start.17 = (f32[48,3072]{1,0:T(8,128)S(1)}, f32[48,3072]{1,0:T(8,128)S(1)}, u32[]{:S(2)}, u32[]{:S(2)}) collective-permute-start(f32[48,3072]{1,0:T(8,128)S(1)} %get-tuple-element.121), channel_id=1, source_target_pairs={{0,24},{8,0},{16,8},{24,16},{1,25},{9,1},{17,9},{25,17},{2,26},{10... | collective-permute-start | bytes 1769480 | tf_op jit(solution)/shard_map/ppermute | solution.py:572
  223.7 2.7 %collective-permute-done.14 = f32[48,3072]{1,0:T(8,128)S(1)} collective-permute-done((f32[48,3072]{1,0:T(8,128)S(1)}, f32[48,3072]{1,0:T(8,128)S(1)}, u32[]{:S(2)}, u32[]{:S(2)}) %collective-permute-start.14) | collective-permute-done | bytes 589856 | tf_op jit(solution)/shard_map/ppermute | solution.py:572
  226.6 3.3 %collective-permute-start.19 = (f32[48,3072]{1,0:T(8,128)S(1)}, f32[48,3072]{1,0:T(8,128)S(1)}, u32[]{:S(2)}, u32[]{:S(2)}) collective-permute-start(f32[48,3072]{1,0:T(8,128)S(1)} %add.31), channel_id=1, source_target_pairs={{0,24},{8,0},{16,8},{24,16},{1,25},{9,1},{17,9},{25,17},{2,26},{10... | collective-permute-start | bytes 1769480 | tf_op jit(solution)/shard_map/ppermute | solution.py:572
  229.9 4.7 %gamma_own.1 = f32[96,3072]{1,0:T(8,128)S(1)} custom-call(s32[2,6]{1,0:T(2,128)S(1)} %bitcast.16, f32[3]{0:T(128)S(1)} %copy-done.2, f32[12,128]{1,0:T(8,128)S(1)} %get-tuple-element.99.refs_2_, f32[96,3072]{1,0:T(8,128)S(1)} %unpack_fitted.1.refs_3_.refs_8_, f32[32,3072]{1,0:T(8,128)S(1)} %collective-permute-done.11.refs_4_.refs_5_, ...), custom_call_target="tpu_custom_call" | custom-call | flops 452984832 | bytes 3538944 | tf_op jit(solution)/shard_map/gamma_own/pallas_call | solution.py:542
  234.6 4.5 %collective-permute-done.16 = f32[48,3072]{1,0:T(8,128)S(1)} collective-permute-done((f32[48,3072]{1,0:T(8,128)S(1)}, f32[48,3072]{1,0:T(8,128)S(1)}, u32[]{:S(2)}, u32[]{:S(2)}) %collective-permute-start.16) | collective-permute-done | bytes 589856 | tf_op jit(solution)/shard_map/ppermute | solution.py:572
  239.1 8.6 %collective-permute-done.15 = f32[48,3072]{1,0:T(8,128)S(1)} collective-permute-done((f32[48,3072]{1,0:T(8,128)S(1)}, f32[48,3072]{1,0:T(8,128)S(1)}, u32[]{:S(2)}, u32[]{:S(2)}) %collective-permute-start.15) | collective-permute-done | bytes 589856 | tf_op jit(solution)/shard_map/ppermute | solution.py:572
  (54 shorter events, 22.0 us)
Async XLA Ops:
  0.1 8.0 %copy-start.3 = (s32[12,4]{0,1:T(4,128)S(1)}, s32[12,4]{0,1:T(4,128)}, u32[]{:S(2)}) copy-start(s32[12,4]{0,1:T(4,128)} %param.11) | copy-start | bytes 580
  3.4 4.7 %collective-permute-start = (f32[2,96,3072]{2,1,0:T(8,128)S(1)}, f32[2,96,3072]{2,1,0:T(8,128)}, u32[]{:S(2)}, u32[]{:S(2)}) collective-permute-start(f32[2,96,3072]{2,1,0:T(8,128)S(1)} %gift_rows.1), channel_id=1, source_target_pairs={{0,32},{32,0},{1,33},{33,1},{2,34},{34,2},{3,35},{35,3},{4,36},{36... | collective-permute-start | bytes 7077896 | tf_op jit(solution)/shard_map/ppermute | solution.py:584
  15.0 76.4 %all-to-all-start.2 = ((f32[64,152,128]{2,1,0:T(8,128)}), f32[64,152,128]{2,1,0:T(8,128)}, u32[]{:S(2)}, u32[]{:S(2)}) async-start(f32[64,152,128]{2,1,0:T(8,128)} %bitcast.23), calls=%async_computation.2 | async-start | bytes 9961472 | tf_op jit(solution)/shard_map/cond/branch_2_fun/all_to_all | solution.py:591
  129.5 47.7 %copy-start = (s32[6,2]{0,1:T(2,128)S(1)}, s32[6,2]{0,1:T(2,128)}, u32[]{:S(2)}) copy-start(s32[6,2]{0,1:T(2,128)} %param.16) | copy-start | bytes 148
  129.5 47.7 %copy-start.2 = (f32[3]{0:T(128)S(1)}, f32[3]{0:T(128)}, u32[]{:S(2)}) copy-start(f32[3]{0:T(128)} %refs_1_.9) | copy-start | bytes 40
  129.5 27.7 %collective-permute-start.5 = (f32[96,3072]{1,0:T(8,128)S(1)}, f32[96,3072]{1,0:T(8,128)S(1)}, u32[]{:S(2)}, u32[]{:S(2)}) collective-permute-start(f32[96,3072]{1,0:T(8,128)S(1)} %unpack_fitted.1.refs_3_.refs_8_), channel_id=1, source_target_pairs={{0,1},{1,0},{2,3},{3,2},{4,5},{5,4},{6,7},{7,6},{8,9},{9,8},{10,11... | collective-permute-start | bytes 3538952 | tf_op jit(solution)/shard_map/ppermute | solution.py:572
  130.3 27.5 %collective-permute-start.4 = (f32[96,3072]{1,0:T(8,128)S(1)}, f32[96,3072]{1,0:T(8,128)S(1)}, u32[]{:S(2)}, u32[]{:S(2)}) collective-permute-start(f32[96,3072]{1,0:T(8,128)S(1)} %unpack_fitted.1.refs_3_.refs_8_), channel_id=1, source_target_pairs={{0,2},{2,4},{4,6},{6,0},{1,3},{3,5},{5,7},{7,1},{8,10},{10,12},{12... | collective-permute-start | bytes 3538952 | tf_op jit(solution)/shard_map/ppermute | solution.py:572
  130.9 27.0 %collective-permute-start.3 = (f32[96,3072]{1,0:T(8,128)S(1)}, f32[96,3072]{1,0:T(8,128)S(1)}, u32[]{:S(2)}, u32[]{:S(2)}) collective-permute-start(f32[96,3072]{1,0:T(8,128)S(1)} %unpack_fitted.1.refs_3_.refs_8_), channel_id=1, source_target_pairs={{0,6},{2,0},{4,2},{6,4},{1,7},{3,1},{5,3},{7,5},{8,14},{10,8},{12,... | collective-permute-start | bytes 3538952 | tf_op jit(solution)/shard_map/ppermute | solution.py:572
  133.6 27.0 %collective-permute-start.2 = (f32[96,3072]{1,0:T(8,128)S(1)}, f32[96,3072]{1,0:T(8,128)S(1)}, u32[]{:S(2)}, u32[]{:S(2)}) collective-permute-start(f32[96,3072]{1,0:T(8,128)S(1)} %unpack_fitted.1.refs_3_.refs_8_), channel_id=1, source_target_pairs={{0,8},{8,16},{16,24},{24,0},{1,9},{9,17},{17,25},{25,1},{2,10},{10... | collective-permute-start | bytes 3538952 | tf_op jit(solution)/shard_map/ppermute | solution.py:572
  134.2 26.4 %collective-permute-start.1 = (f32[96,3072]{1,0:T(8,128)S(1)}, f32[96,3072]{1,0:T(8,128)S(1)}, u32[]{:S(2)}, u32[]{:S(2)}) collective-permute-start(f32[96,3072]{1,0:T(8,128)S(1)} %unpack_fitted.1.refs_3_.refs_8_), channel_id=1, source_target_pairs={{0,24},{8,0},{16,8},{24,16},{1,25},{9,1},{17,9},{25,17},{2,26},{10... | collective-permute-start | bytes 3538952 | tf_op jit(solution)/shard_map/ppermute | solution.py:572
  160.6 29.0 %collective-permute-start.7 = (f32[96,3072]{1,0:T(8,128)S(1)}, f32[96,3072]{1,0:T(8,128)S(1)}, u32[]{:S(2)}, u32[]{:S(2)}) collective-permute-start(f32[96,3072]{1,0:T(8,128)S(1)} %collective-permute-done.5.refs_11_), channel_id=1, source_target_pairs={{0,6},{2,0},{4,2},{6,4},{1,7},{3,1},{5,3},{7,5},{8,14},{10,8},{12,... | collective-permute-start | bytes 3538952 | tf_op jit(solution)/shard_map/ppermute | solution.py:572
  160.9 28.8 %collective-permute-start.8 = (f32[96,3072]{1,0:T(8,128)S(1)}, f32[96,3072]{1,0:T(8,128)S(1)}, u32[]{:S(2)}, u32[]{:S(2)}) collective-permute-start(f32[96,3072]{1,0:T(8,128)S(1)} %collective-permute-done.4.refs_10_), channel_id=1, source_target_pairs={{0,1},{1,0},{2,3},{3,2},{4,5},{5,4},{6,7},{7,6},{8,9},{9,8},{10,11... | collective-permute-start | bytes 3538952 | tf_op jit(solution)/shard_map/ppermute | solution.py:572
  163.2 26.5 %collective-permute-start.6 = (f32[96,3072]{1,0:T(8,128)S(1)}, f32[96,3072]{1,0:T(8,128)S(1)}, u32[]{:S(2)}, u32[]{:S(2)}) collective-permute-start(f32[96,3072]{1,0:T(8,128)S(1)} %collective-permute-done.4.refs_10_), channel_id=1, source_target_pairs={{0,2},{2,4},{4,6},{6,0},{1,3},{3,5},{5,7},{7,1},{8,10},{10,12},{12... | collective-permute-start | bytes 3538952 | tf_op jit(solution)/shard_map/ppermute | solution.py:572
  165.0 12.2 %collective-permute-start.10 = (f32[48,3072]{1,0:T(8,128)S(1)}, f32[48,3072]{1,0:T(8,128)S(1)}, u32[]{:S(2)}, u32[]{:S(2)}) collective-permute-start(f32[48,3072]{1,0:T(8,128)S(1)} %slice.20), channel_id=1, source_target_pairs={{0,8},{8,16},{16,24},{24,0},{1,9},{9,17},{17,25},{25,1},{2,10},{10... | collective-permute-start | bytes 1769480 | tf_op jit(solution)/shard_map/ppermute | solution.py:572
  165.1 12.2 %collective-permute-start.9 = (f32[48,3072]{1,0:T(8,128)S(1)}, f32[48,3072]{1,0:T(8,128)S(1)}, u32[]{:S(2)}, u32[]{:S(2)}) collective-permute-start(f32[48,3072]{1,0:T(8,128)S(1)} %slice.19), channel_id=1, source_target_pairs={{0,24},{8,0},{16,8},{24,16},{1,25},{9,1},{17,9},{25,17},{2,26},{10... | collective-permute-start | bytes 1769480 | tf_op jit(solution)/shard_map/ppermute | solution.py:572
  189.7 16.5 %collective-permute-start.11 = (f32[32,3072]{1,0:T(8,128)S(1)}, f32[32,3072]{1,0:T(8,128)S(1)}, u32[]{:S(2)}, u32[]{:S(2)}) collective-permute-start(f32[32,3072]{1,0:T(8,128)S(1)} %slice.21), channel_id=1, source_target_pairs={{0,1},{1,0},{2,3},{3,2},{4,5},{5,4},{6,7},{7,6},{8,9},{9,8},{10,11... | collective-permute-start | bytes 1179656 | tf_op jit(solution)/shard_map/ppermute | solution.py:572
  191.5 14.8 %collective-permute-start.12 = (f32[32,3072]{1,0:T(8,128)S(1)}, f32[32,3072]{1,0:T(8,128)S(1)}, u32[]{:S(2)}, u32[]{:S(2)}) collective-permute-start(f32[32,3072]{1,0:T(8,128)S(1)} %slice.22), channel_id=1, source_target_pairs={{0,6},{2,0},{4,2},{6,4},{1,7},{3,1},{5,3},{7,5},{8,14},{10,8},{12,... | collective-permute-start | bytes 1179656 | tf_op jit(solution)/shard_map/ppermute | solution.py:572
  193.3 13.0 %collective-permute-start.13 = (f32[32,3072]{1,0:T(8,128)S(1)}, f32[32,3072]{1,0:T(8,128)S(1)}, u32[]{:S(2)}, u32[]{:S(2)}) collective-permute-start(f32[32,3072]{1,0:T(8,128)S(1)} %slice.23), channel_id=1, source_target_pairs={{0,2},{2,4},{4,6},{6,0},{1,3},{3,5},{5,7},{7,1},{8,10},{10,12},{12... | collective-permute-start | bytes 1179656 | tf_op jit(solution)/shard_map/ppermute | solution.py:572
  211.1 15.3 %collective-permute-start.14 = (f32[48,3072]{1,0:T(8,128)S(1)}, f32[48,3072]{1,0:T(8,128)S(1)}, u32[]{:S(2)}, u32[]{:S(2)}) collective-permute-start(f32[48,3072]{1,0:T(8,128)S(1)} %get-tuple-element.119), channel_id=1, source_target_pairs={{0,8},{8,16},{16,24},{24,0},{1,9},{9,17},{17,25},{25,1},{2,10},{10... | collective-permute-start | bytes 1769480 | tf_op jit(solution)/shard_map/ppermute | solution.py:572
  212.1 14.5 %collective-permute-start.18 = (f32[48,3072]{1,0:T(8,128)S(1)}, f32[48,3072]{1,0:T(8,128)S(1)}, u32[]{:S(2)}, u32[]{:S(2)}) collective-permute-start(f32[48,3072]{1,0:T(8,128)S(1)} %get-tuple-element.123), channel_id=1, source_target_pairs={{0,24},{8,0},{16,8},{24,16},{1,25},{9,1},{17,9},{25,17},{2,26},{10... | collective-permute-start | bytes 1769480 | tf_op jit(solution)/shard_map/ppermute | solution.py:572
  220.4 18.6 %collective-permute-start.16 = (f32[48,3072]{1,0:T(8,128)S(1)}, f32[48,3072]{1,0:T(8,128)S(1)}, u32[]{:S(2)}, u32[]{:S(2)}) collective-permute-start(f32[48,3072]{1,0:T(8,128)S(1)} %get-tuple-element.120), channel_id=1, source_target_pairs={{0,8},{8,16},{16,24},{24,0},{1,9},{9,17},{17,25},{25,1},{2,10},{10... | collective-permute-start | bytes 1769480 | tf_op jit(solution)/shard_map/ppermute | solution.py:572
  220.5 18.7 %collective-permute-start.17 = (f32[48,3072]{1,0:T(8,128)S(1)}, f32[48,3072]{1,0:T(8,128)S(1)}, u32[]{:S(2)}, u32[]{:S(2)}) collective-permute-start(f32[48,3072]{1,0:T(8,128)S(1)} %get-tuple-element.121), channel_id=1, source_target_pairs={{0,24},{8,0},{16,8},{24,16},{1,25},{9,1},{17,9},{25,17},{2,26},{10... | collective-permute-start | bytes 1769480 | tf_op jit(solution)/shard_map/ppermute | solution.py:572
  226.5 21.3 %collective-permute-start.15 = (f32[48,3072]{1,0:T(8,128)S(1)}, f32[48,3072]{1,0:T(8,128)S(1)}, u32[]{:S(2)}, u32[]{:S(2)}) collective-permute-start(f32[48,3072]{1,0:T(8,128)S(1)} %add.29), channel_id=1, source_target_pairs={{0,8},{8,16},{16,24},{24,0},{1,9},{9,17},{17,25},{25,1},{2,10},{10... | collective-permute-start | bytes 1769480 | tf_op jit(solution)/shard_map/ppermute | solution.py:572
  226.6 21.1 %collective-permute-start.19 = (f32[48,3072]{1,0:T(8,128)S(1)}, f32[48,3072]{1,0:T(8,128)S(1)}, u32[]{:S(2)}, u32[]{:S(2)}) collective-permute-start(f32[48,3072]{1,0:T(8,128)S(1)} %add.31), channel_id=1, source_target_pairs={{0,24},{8,0},{16,8},{24,16},{1,25},{9,1},{17,9},{25,17},{2,26},{10... | collective-permute-start | bytes 1769480 | tf_op jit(solution)/shard_map/ppermute | solution.py:572
  (2 other events, 6.9 us)
